TPU v7x, 128 devices: a whole 4x4x4 slice. The times are simulated.
128 devices in a mesh: win: 4 (over y_lo, core), srow: 4 (over x), scol: 8 (over z, y_hi).
Axes of the slice: x: 4, y: 4 (y_hi: 2, y_lo: 2; y = y_hi * 2 + y_lo), z: 4, core: 2. Of those that a mesh axis runs over, the one named last changes fastest.
Arguments:
- spectra: float32 [4, 2, 64, 4096], P(None, None, 'win', ('srow', 'scol')), may hold values from -6 to 6
- bins: int32 [4], replicated, may hold values from 1 to 2047
- travel: int32 [4096, 2048], P(('srow', 'scol'), 'win'), may hold values from 0 to 16383
Outputs:
- coherence: bfloat16 [4, 2, 4096, 4, 1024], P('win', None, 'srow', None, 'scol')
- beam: float32 [4, 2048], P('win')
All inputs are finite; a program needn't handle non-finite values.
Results may differ from a plain program's by a relative error of at most 0.012.
Values may be sent and summed in bfloat16 or wider, within the bound.
No kernel may reach another device: no remote copies, remote signals or barrier semaphores. Data moves between devices by JAX's collectives and lax.ppermute only.
A program may use at most 128 MiB of HBM per device.

v0:
```python
import jax
import jax.numpy as jnp
from jax import lax
from jax.experimental import pallas as pl
from jax.experimental.pallas import tpu as pltpu
from jax.sharding import PartitionSpec as P


S = 4096
NFFT = 4096
F = 4
NST = 128
NPT = 512
ALL = ("win", "srow", "scol")
ROW_OFF = (0, 1, 2, -3, 4)
WEIGHT = ((1, 2, 1), (2, 2, 2, 2), (2, 2, 2, 2), (2, 2, 2, 2), (1, 2, 1))
RELAY = (4, 6, 7)
SENDS = (('srow', 3), ('srow', 2), ('scol', 2), ('srow', 1), ('scol', 4), ('scol', -3), ('scol', 1))
ROUND = 12582912.0
AHEAD = 1

ROOT2 = 2.0**0.5
SIN = [ROOT2 * v for v in (3.141592580044453, -5.167706878911761, 2.5500313770692338,
                           -0.5980451729935192, 0.07722012694435497)]
COS = [-ROOT2 * v for v in (0.9999999534664096, -4.93479285864205, 4.058411913501759,
                            -1.331880156986464, 0.2196967900729894)]


def prep_kernel(spectra_hbm, travel_hbm, bins_hbm, payload, scales, spectra, travel, bins, sems):
    moves = [
        pltpu.make_async_copy(spectra_hbm, spectra, sems.at[0]),
        pltpu.make_async_copy(travel_hbm, travel, sems.at[1]),
        pltpu.make_async_copy(bins_hbm, bins, sems.at[2]),
    ]
    for move in moves:
        move.start()
    moves[0].wait()
    for f in range(F):
        re = spectra[f, 0]
        im = spectra[f, 1]
        magnitude = jnp.sqrt(re * re + im * im + 0.5)
        for c, part in enumerate((re, im)):
            value = (part / magnitude).astype(jnp.bfloat16).astype(jnp.float32) * 32768.0
            value = jnp.clip((value + ROUND) - ROUND, -32767.0, 32767.0)
            at = NPT + 32 * f + 16 * c
            payload[at:at + 16, :] = value.astype(jnp.int32).astype(jnp.int16)
    moves[1].wait()
    payload[0:NPT, :] = travel[...].T.astype(jnp.int16)
    moves[2].wait()
    for f in range(F):
        scales[f] = jnp.full((8, NST), bins[f].astype(jnp.float32) * (1.0 / NFFT), jnp.float32)


def on_chip(*arrays):
    return [pltpu.with_memory_space_constraint(v, pltpu.VMEM) for v in arrays]


def vmem(n):
    return [pl.BlockSpec(memory_space=pltpu.VMEM)] * n


SMEM = pl.BlockSpec(memory_space=pltpu.SMEM)
LIMIT = pltpu.CompilerParams(vmem_limit_bytes=16 * 2**20)


def steer_kernel(scales, *refs):
    payloads, out = refs[:-1], refs[-1]
    rows = 64
    for n, ref in enumerate(payloads):
        def chunk(i, carry, n=n, ref=ref):
            at = pl.ds(pl.multiple_of(i * rows, rows), rows)
            samples = (ref[at, :].astype(jnp.int32) & (NFFT - 1)).astype(jnp.float32)
            for f in range(F):
                turns = (samples.reshape(rows // 8, 8, NST) * scales[f]).reshape(rows, NST)
                r = turns - lax.round(turns, lax.RoundingMethod.TO_NEAREST_EVEN)
                z = r * r
                s = SIN[4]
                c = COS[4]
                for k in (3, 2, 1, 0):
                    s = s * z + SIN[k]
                    c = c * z + COS[k]
                s = s * r
                out[f, 0, n, at, :] = (1.0 - s * s).astype(jnp.bfloat16)
                out[f, 1, n, at, :] = (s * c).astype(jnp.bfloat16)
            return carry

        lax.fori_loop(0, NPT // rows, chunk, 0)


def steer(scales, payloads):
    n = len(payloads)
    return pl.pallas_call(
        steer_kernel,
        out_shape=pltpu.VMEM((F, 2, n, NPT, NST), jnp.bfloat16),
        in_specs=vmem(n + 1),
        out_specs=vmem(1)[0],
        compiler_params=LIMIT,
    )(*on_chip(scales, *payloads))


def stack_kernel(*refs):
    for n, ref in enumerate(refs[:-1]):
        refs[-1][n] = ref[NPT:NPT + 32 * F, :]


def stack(payloads):
    return pl.pallas_call(
        stack_kernel,
        out_shape=pltpu.VMEM((len(payloads), 32 * F, NST), jnp.int16),
        in_specs=vmem(len(payloads)),
        out_specs=vmem(1)[0],
        compiler_params=LIMIT,
        name="stack",
    )(*on_chip(*payloads))


def decode(sources, block, f):
    at = slice(32 * f, 32 * f + 32) if isinstance(f, int) else pl.ds(pl.multiple_of(32 * f, 32), 32)
    return [
        (a[block, at, :].astype(jnp.int32).astype(jnp.float32) * (1.0 / 32768.0)).astype(jnp.bfloat16)
        for a in sources
    ]


def beam_kernel(own_steer, col_steer, row_steer, a0, a1, a2, a3, beam, cols, weights):
    sources = (a0, a1, a2, a3)

    def coherent(f, k):
        if k == 0:
            for d in range(4):
                cols[f % 2, d * NST:(d + 1) * NST, :] = jnp.concatenate(decode(sources, d, f), axis=0).T
        parts = decode(sources, 0 if k == 0 else 3 + k, f)
        x = jnp.concatenate(parts, axis=0)
        z = jnp.concatenate([q for v in parts for q in (v[16:32], -v[0:16])], axis=0)
        right = jnp.concatenate([x, z], axis=1)
        for j, weight in enumerate(WEIGHT[k]):
            at = slice(j * NST, (j + 1) * NST)
            cross = jnp.dot(cols[f % 2, at, :], right, preferred_element_type=jnp.float32)
            re = cross[:, :NST]
            im = cross[:, NST:]
            inverse = lax.rsqrt(re * re + im * im + 64.0)
            if weight == 2:
                inverse = inverse + inverse
            re = (re * inverse).astype(jnp.bfloat16)
            im = (im * inverse).astype(jnp.bfloat16)
            at = slice(2 * j * NST, (2 * j + 1) * NST)
            weights[k, at, :NST] = re
            weights[k, at, NST:] = im
            at = slice((2 * j + 1) * NST, (2 * j + 2) * NST)
            weights[k, at, :NST] = -im
            weights[k, at, NST:] = re

    def product(f, k):
        depth = len(WEIGHT[k])
        steer_cols = jnp.concatenate(
            ([own_steer[f, 0, 0], own_steer[f, 1, 0]] + [row_steer[f, part, n] for n in range(3) for part in range(2)])[:2 * depth],
            axis=1,
        )
        image = jnp.dot(steer_cols, weights[k, :2 * NST * depth], preferred_element_type=jnp.float32)
        re, im = (own_steer[f, 0, 0], own_steer[f, 1, 0]) if k == 0 else (col_steer[f, 0, k - 1], col_steer[f, 1, k - 1])
        return re.astype(jnp.float32) * image[:, :NST] + im.astype(jnp.float32) * image[:, NST:]

    steps = [(f, k) for f in range(F) for k in range(5)]
    for step in steps[:AHEAD]:
        coherent(*step)
    for n, (f, k) in enumerate(steps):
        if n + AHEAD < len(steps):
            coherent(*steps[n + AHEAD])
        power = product(f, k)
        total = power if k == 0 else total + power
        if k == 4:
            values = [
                jnp.sum(total[j * NST:(j + 1) * NST, :].T, axis=0, keepdims=True) * (1.0 / S) for j in range(4)
            ]
            beam[f] = jnp.broadcast_to(jnp.concatenate(values, axis=0)[None], (32, 4, NST)).astype(jnp.bfloat16)


def beams(own_steer, col_steer, row_steer, spectra):
    return pl.pallas_call(
        beam_kernel,
        out_shape=pltpu.VMEM((F, 32, 4, NST), jnp.bfloat16),
        in_specs=vmem(7),
        out_specs=vmem(1)[0],
        scratch_shapes=[
            pltpu.VMEM((2, 4 * NST, NST), jnp.bfloat16),
            pltpu.VMEM((5, 8 * NST, 2 * NST), jnp.bfloat16),
        ],
        compiler_params=LIMIT,
        name="beams",
    )(*on_chip(own_steer, col_steer, row_steer, *spectra))


def pack_kernel(a0, a1, a2, a3, rows):
    at = pl.ds(pl.multiple_of(32 * lax.axis_index("win"), 32), 32)
    for s, a in enumerate((a0, a1, a2, a3)):
        for n, block in enumerate(RELAY):
            rows[s, n] = a[block, at, :]


def pack(spectra):
    return pl.pallas_call(
        pack_kernel,
        out_shape=pltpu.VMEM((4, 3, 32, NST), jnp.int16),
        in_specs=vmem(4),
        out_specs=vmem(1)[0],
        compiler_params=LIMIT,
        name="pack",
    )(*on_chip(*spectra))


def fill_columns(sources, f, cols):
    for d in range(4):
        parts = decode(sources, d, f)
        x = jnp.concatenate(parts, axis=0)
        y = jnp.concatenate([q for v in parts for q in (-v[16:32], v[0:16])], axis=0)
        cols[d] = jnp.concatenate([x, y], axis=1)


def emit(parts, cols, r, scratch, ready):
    left = jnp.concatenate(parts, axis=0).T
    for d in range(4):
        cross = jnp.dot(left, cols[d], preferred_element_type=jnp.float32)
        re = cross[:, :NST]
        im = cross[:, NST:]
        inverse = lax.rsqrt(re * re + im * im + 64.0)
        at = pl.ds((r + d) & 3, NST, stride=4)
        scratch[0, at, :] = re * inverse
        scratch[1, at, :] = im * inverse
    ready[0] = scratch[0].astype(jnp.bfloat16)
    ready[1] = scratch[1].astype(jnp.bfloat16)


def block_copy(ready, coherence, offset, sem):
    row = (lax.axis_index("scol") + offset) & 7
    at = pl.ds(pl.multiple_of(row * (4 * NST), 4 * NST), 4 * NST)
    return pltpu.make_async_copy(ready, coherence.at[:, at, :], sem)


def near_kernel(a0, a1, a2, a3, coherence, cols, scratch, ready, sems):
    w, r = lax.axis_index("win"), lax.axis_index("srow")
    sources = (a0, a1, a2, a3)
    fill_columns(sources, w, cols)
    for n, offset in enumerate(ROW_OFF):
        emit(decode(sources, 0 if n == 0 else 3 + n, w), cols, r, scratch, ready.at[n])
        block_copy(ready.at[n], coherence, offset, sems.at[n]).start()
    for n, offset in enumerate(ROW_OFF):
        block_copy(ready.at[n], coherence, offset, sems.at[n]).wait()


def far_kernel(rows, a0, a1, a2, a3, old, coherence, cols, scratch, ready, sems):
    w, r = lax.axis_index("win"), lax.axis_index("srow")
    fill_columns((a0, a1, a2, a3), w, cols)
    for n, offset in enumerate((3, -1, -2)):
        emit(decode([rows.at[k] for k in range(4)], n, 0), cols, r, scratch, ready.at[n])
        block_copy(ready.at[n], coherence, offset, sems.at[n]).start()
    for n, offset in enumerate((3, -1, -2)):
        block_copy(ready.at[n], coherence, offset, sems.at[n]).wait()


def tile_scratch(n):
    return [
        pltpu.VMEM((4, NST, 2 * NST), jnp.bfloat16),
        pltpu.VMEM((2, 4 * NST, NST), jnp.float32),
        pltpu.VMEM((n, 2, 4 * NST, NST), jnp.bfloat16),
        pltpu.SemaphoreType.DMA((n,)),
    ]


TILE = jax.ShapeDtypeStruct((2, 4 * 1024, NST), jnp.bfloat16)
ANY = pl.BlockSpec(memory_space=pl.ANY)


def near_tile(spectra):
    return pl.pallas_call(
        near_kernel,
        in_specs=vmem(4),
        out_specs=ANY,
        scratch_shapes=tile_scratch(5),
        out_shape=TILE,
        compiler_params=LIMIT,
        name="near",
    )(*on_chip(*spectra))


def far_tile(rows, spectra, coherence):
    return pl.pallas_call(
        far_kernel,
        in_specs=vmem(5) + [ANY],
        out_specs=ANY,
        scratch_shapes=tile_scratch(3),
        out_shape=TILE,
        input_output_aliases={5: 0},
        compiler_params=LIMIT,
        name="far",
    )(*on_chip(rows, *spectra), coherence)


def from_offset(value, axis, offset):
    size = lax.axis_size(axis)
    return lax.ppermute(value, axis, [((i + offset) % size, i) for i in range(size)])


def from_partner(value, bit):
    return lax.ppermute(value, "win", [(i ^ bit, i) for i in range(4)])


def body(spectra, bins, travel):
    return local(spectra, bins, travel)


def local(spectra, bins, travel):
    return local(spectra, bins, travel)


def local(spectra, bins, travel):
    payload, scales = pl.pallas_call(
        prep_kernel,
        out_shape=(
            pltpu.VMEM((NPT + 32 * F, NST), jnp.int16),
            pltpu.VMEM((F, 8, NST), jnp.float32),
        ),
        in_specs=[ANY] * 3,
        out_specs=tuple(vmem(2)),
        scratch_shapes=[
            pltpu.VMEM(spectra.shape, jnp.float32),
            pltpu.VMEM(travel.shape, jnp.int32),
            pltpu.SMEM((F,), jnp.int32),
            pltpu.SemaphoreType.DMA((3,)),
        ],
        compiler_params=LIMIT,
        name="prep",
    )(*(pltpu.with_memory_space_constraint(v, pltpu.HBM) for v in (spectra, travel, bins)))
    got = {}
    for axis, offset in SENDS:
        got[axis, offset] = from_offset(payload, axis, offset)
    by_row = [got["srow", d] for d in (1, 2, 3)]
    by_col = [got["scol", d] for d in ROW_OFF[1:]]
    steer0 = steer(scales, [payload])
    steer2 = steer(scales, by_row)
    by_col, steer0, steer2 = lax.optimization_barrier((by_col, steer0, steer2))
    a0 = stack([payload] + by_row + by_col)
    a1 = from_partner(a0, 2)
    steer1 = steer(scales, by_col)
    a0, steer1 = lax.optimization_barrier((a0, steer1))
    a2 = from_partner(a0, 1)
    a1, steer1 = lax.optimization_barrier((a1, steer1))
    a3 = from_partner(a1, 1)
    sources = (a0, a1, a2, a3)
    packed = pack(sources)
    rows = from_offset(packed, "scol", 2)
    partial = beams(steer0, steer1, steer2, sources)
    shares = lax.all_to_all(partial.reshape(128, 4, NST), ALL, 0, 0, tiled=True)
    coherence = far_tile(rows, sources, near_tile(sources))
    beam = shares.astype(jnp.float32).reshape(4, 32, 4, NST).sum(axis=1).reshape(1, 4 * NPT)
    return coherence.reshape(1, 2, 1024, 4, NST), beam


def solution(mesh):
    placed = (P(None, None, "win", ("srow", "scol")), P(), P(("srow", "scol"), "win"))
    return jax.shard_map(
        body,
        mesh=mesh,
        in_specs=placed,
        out_specs=(P("win", None, "srow", None, "scol"), P("win", None)),
        check_vma=False,
    )
```

profile of v0, /device:TPU:0, one launch (start us, length us, event | category | flops | bytes accessed | tf_op | source)
XLA Modules:
  0.0 57.1 jit_solution(9746307149832011995)
XLA Ops:
  0.6 1.2 %prep.1 = (s16[640,128]{1,0:T(8,128)(2,1)S(1)}, f32[4,8,128]{2,1,0:T(8,128)S(1)}) custom-call(f32[4,2,16,128]{3,2,1,0:T(8,128)} %spectra_hbm.1, s32[128,512]{1,0:T(8,128)} %travel_hbm.1, s32[4]{0:T(128)} %bins_hbm.1), custom_call_target="tpu_custom_call" | custom-call | tf_op jit(solution)/shard_map/prep/pallas_call | solution.py:316
  1.8 1.7 %collective-permute-start.2 = (s16[640,128]{1,0:T(8,128)(2,1)S(1)}, s16[640,128]{1,0:T(8,128)(2,1)S(1)}, u32[]{:S(2)}, u32[]{:S(2)}) collective-permute-start(s16[640,128]{1,0:T(8,128)(2,1)S(1)} %get-tuple-element.14.refs_0_), channel_id=1, source_target_pairs={{24,0},{0,8},{8,16},{16,24},{25,1},{1,9},{9,17},{17,25},{26,2},{2,... | collective-permute-start | bytes 491528 | tf_op jit(solution)/shard_map/ppermute | solution.py:300
  3.5 2.7 %collective-permute-start.1 = (s16[640,128]{1,0:T(8,128)(2,1)S(1)}, s16[640,128]{1,0:T(8,128)(2,1)S(1)}, u32[]{:S(2)}, u32[]{:S(2)}) collective-permute-start(s16[640,128]{1,0:T(8,128)(2,1)S(1)} %get-tuple-element.14.refs_0_), channel_id=1, source_target_pairs={{16,0},{24,8},{0,16},{8,24},{17,1},{25,9},{1,17},{9,25},{18,2},{26... | collective-permute-start | bytes 491528 | tf_op jit(solution)/shard_map/ppermute | solution.py:300
  6.2 3.9 %collective-permute-start.6 = (s16[640,128]{1,0:T(8,128)(2,1)S(1)}, s16[640,128]{1,0:T(8,128)(2,1)S(1)}, u32[]{:S(2)}, u32[]{:S(2)}) collective-permute-start(s16[640,128]{1,0:T(8,128)(2,1)S(1)} %get-tuple-element.14.refs_0_), channel_id=1, source_target_pairs={{4,0},{5,1},{6,2},{7,3},{0,4},{1,5},{2,6},{3,7},{12,8},{13,9},{14,... | collective-permute-start | bytes 491528 | tf_op jit(solution)/shard_map/ppermute | solution.py:300
  10.1 1.4 %collective-permute-start = (s16[640,128]{1,0:T(8,128)(2,1)S(1)}, s16[640,128]{1,0:T(8,128)(2,1)S(1)}, u32[]{:S(2)}, u32[]{:S(2)}) collective-permute-start(s16[640,128]{1,0:T(8,128)(2,1)S(1)} %get-tuple-element.14.refs_0_), channel_id=1, source_target_pairs={{8,0},{16,8},{24,16},{0,24},{9,1},{17,9},{25,17},{1,25},{10,2},{18... | collective-permute-start | bytes 491528 | tf_op jit(solution)/shard_map/ppermute | solution.py:300
  11.5 3.6 %collective-permute-start.5 = (s16[640,128]{1,0:T(8,128)(2,1)S(1)}, s16[640,128]{1,0:T(8,128)(2,1)S(1)}, u32[]{:S(2)}, u32[]{:S(2)}) collective-permute-start(s16[640,128]{1,0:T(8,128)(2,1)S(1)} %get-tuple-element.14.refs_0_), channel_id=1, source_target_pairs={{5,0},{6,1},{7,2},{0,3},{1,4},{2,5},{3,6},{4,7},{13,8},{14,9},{15,... | collective-permute-start | bytes 491528 | tf_op jit(solution)/shard_map/ppermute | solution.py:300
  15.2 2.2 %collective-permute-start.4 = (s16[640,128]{1,0:T(8,128)(2,1)S(1)}, s16[640,128]{1,0:T(8,128)(2,1)S(1)}, u32[]{:S(2)}, u32[]{:S(2)}) collective-permute-start(s16[640,128]{1,0:T(8,128)(2,1)S(1)} %get-tuple-element.14.refs_0_), channel_id=1, source_target_pairs={{2,0},{3,1},{4,2},{5,3},{6,4},{7,5},{0,6},{1,7},{10,8},{11,9},{12,... | collective-permute-start | bytes 491528 | tf_op jit(solution)/shard_map/ppermute | solution.py:300
  17.4 2.9 %collective-permute-start.3 = (s16[640,128]{1,0:T(8,128)(2,1)S(1)}, s16[640,128]{1,0:T(8,128)(2,1)S(1)}, u32[]{:S(2)}, u32[]{:S(2)}) collective-permute-start(s16[640,128]{1,0:T(8,128)(2,1)S(1)} %get-tuple-element.14.refs_0_), channel_id=1, source_target_pairs={{1,0},{2,1},{3,2},{4,3},{5,4},{6,5},{7,6},{0,7},{9,8},{10,9},{11,1... | collective-permute-start | bytes 491528 | tf_op jit(solution)/shard_map/ppermute | solution.py:300
  20.3 0.9 %shard_map.50.own_steer = bf16[4,2,1,512,128]{4,3,2,1,0:T(8,128)(2,1)S(1)} custom-call(f32[4,8,128]{2,1,0:T(8,128)S(1)} %get-tuple-element.15.scales, s16[640,128]{1,0:T(8,128)(2,1)S(1)} %get-tuple-element.14.refs_0_), custom_call_target="tpu_custom_call" | custom-call | tf_op jit(solution)/shard_map/pallas_call | solution.py:92
  21.3 2.8 %shard_map.51.row_steer = bf16[4,2,3,512,128]{4,3,2,1,0:T(8,128)(2,1)S(1)} custom-call(f32[4,8,128]{2,1,0:T(8,128)S(1)} %get-tuple-element.15.scales, s16[640,128]{1,0:T(8,128)(2,1)S(1)} %collective-permute-done.refs_0_.refs_1_, s16[640,128]{1,0:T(8,128)(2,1)S(1)} %collective-permute-done.1.refs_1_.refs_2_, ...), custom_call_target="tpu_custom_call" | custom-call | tf_op jit(solution)/shard_map/pallas_call | solution.py:92
  24.1 0.1 collective-permute-done.3.refs_4_.refs_0_
  24.2 0.8 %collective-permute-start.7 = (s16[8,128,128]{2,1,0:T(8,128)(2,1)S(1)}, s16[8,128,128]{2,1,0:T(8,128)(2,1)S(1)}, u32[]{:S(2)}, u32[]{:S(2)}) collective-permute-start(s16[8,128,128]{2,1,0:T(8,128)(2,1)S(1)} %stack.1.a0), channel_id=1, source_target_pairs={{64,0},{96,32},{0,64},{32,96},{65,1},{97,33},{1,65},{33,97},{66,2}... | collective-permute-start | bytes 786440 | tf_op jit(solution)/shard_map/ppermute | solution.py:304
  25.0 3.8 %shard_map.52.col_steer = bf16[4,2,4,512,128]{4,3,2,1,0:T(8,128)(2,1)S(1)} custom-call(f32[4,8,128]{2,1,0:T(8,128)S(1)} %get-tuple-element.15.scales, s16[640,128]{1,0:T(8,128)(2,1)S(1)} %collective-permute-done.3.refs_4_.refs_0_, s16[640,128]{1,0:T(8,128)(2,1)S(1)} %collective-permute-done.4.refs_5_.refs_1_, ...), custom_call_target="tpu_custom_call" | custom-call | tf_op jit(solution)/shard_map/pallas_call | solution.py:92
  28.8 0.1 collective-permute-start.8
  28.9 2.3 %collective-permute-done.7.a1 = s16[8,128,128]{2,1,0:T(8,128)(2,1)S(1)} collective-permute-done((s16[8,128,128]{2,1,0:T(8,128)(2,1)S(1)}, s16[8,128,128]{2,1,0:T(8,128)(2,1)S(1)}, u32[]{:S(2)}, u32[]{:S(2)}) %collective-permute-start.7) | collective-permute-done | bytes 262176 | tf_op jit(solution)/shard_map/ppermute | solution.py:304
  31.2 1.5 %collective-permute-done.9.a3 = s16[8,128,128]{2,1,0:T(8,128)(2,1)S(1)} collective-permute-done((s16[8,128,128]{2,1,0:T(8,128)(2,1)S(1)}, s16[8,128,128]{2,1,0:T(8,128)(2,1)S(1)}, u32[]{:S(2)}, u32[]{:S(2)}) %collective-permute-start.9) | collective-permute-done | bytes 262176 | tf_op jit(solution)/shard_map/ppermute | solution.py:304
  32.7 7.4 %beams.1 = bf16[4,32,4,128]{3,2,1,0:T(4,128)(2,1)} custom-call(bf16[4,2,1,512,128]{4,3,2,1,0:T(8,128)(2,1)S(1)} %shard_map.50.own_steer, bf16[4,2,4,512,128]{4,3,2,1,0:T(8,128)(2,1)S(1)} %shard_map.52.col_steer, bf16[4,2,3,512,128]{4,3,2,1,0:T(8,128)(2,1)S(1)} %shard_map.51.row_steer, s16[8,128,128]{2,1,0:T(8,128)(2,1)S(1)} %stack.1.a0, ...), custom_call_target="tpu_custom_call" | custom-call | tf_op jit(solution)/shard_map/beams/pallas_call | solution.py:179
  40.1 6.7 %all-to-all-start = ((bf16[128,4,128]{2,1,0:T(4,128)(2,1)}), bf16[128,4,128]{2,1,0:T(4,128)(2,1)S(1)}, u32[]{:S(2)}, u32[]{:S(2)}) async-start(bf16[128,4,128]{2,1,0:T(4,128)(2,1)} %bitcast.1), calls=%async_computation | async-start | bytes 262144 | tf_op jit(solution)/shard_map/all_to_all | solution.py:352
  46.9 2.9 %collective-permute-start.10 = (s16[4,3,32,128]{3,2,1,0:T(8,128)(2,1)S(1)}, s16[4,3,32,128]{3,2,1,0:T(8,128)(2,1)S(1)}, u32[]{:S(2)}, u32[]{:S(2)}) collective-permute-start(s16[4,3,32,128]{3,2,1,0:T(8,128)(2,1)S(1)} %pack.1), channel_id=1, source_target_pairs={{2,0},{3,1},{4,2},{5,3},{6,4},{7,5},{0,6},{1,7},{10,8},{11,9},{12,... | collective-permute-start | bytes 294920 | tf_op jit(solution)/shard_map/ppermute | solution.py:300
  49.8 1.7 %near.1.old = bf16[2,4096,128]{2,1,0:T(8,128)(2,1)} custom-call(s16[8,128,128]{2,1,0:T(8,128)(2,1)S(1)} %stack.1.a0, s16[8,128,128]{2,1,0:T(8,128)(2,1)S(1)} %collective-permute-done.7.a1, s16[8,128,128]{2,1,0:T(8,128)(2,1)S(1)} %collective-permute-done.8.a2, s16[8,128,128]{2,1,0:T(8,128)(2,1)S(1)} %collective-permute-done.9.a3), custom_call_target="tpu_custom_call" | custom-call | tf_op jit(solution)/shard_map/near/pallas_call | solution.py:274
  51.4 1.4 %collective-permute-done.10.rows = s16[4,3,32,128]{3,2,1,0:T(8,128)(2,1)S(1)} collective-permute-done((s16[4,3,32,128]{3,2,1,0:T(8,128)(2,1)S(1)}, s16[4,3,32,128]{3,2,1,0:T(8,128)(2,1)S(1)}, u32[]{:S(2)}, u32[]{:S(2)}) %collective-permute-start.10) | collective-permute-done | bytes 98336 | tf_op jit(solution)/shard_map/ppermute | solution.py:300
  52.8 1.3 %far.1 = bf16[2,4096,128]{2,1,0:T(8,128)(2,1)} custom-call(s16[4,3,32,128]{3,2,1,0:T(8,128)(2,1)S(1)} %collective-permute-done.10.rows, s16[8,128,128]{2,1,0:T(8,128)(2,1)S(1)} %stack.1.a0, s16[8,128,128]{2,1,0:T(8,128)(2,1)S(1)} %collective-permute-done.7.a1, s16[8,128,128]{2,1,0:T(8,128)(2,1)S(1)} %collective-permute-done.8.a2, ...), custom_call_target="tpu_custom_call", output_to_operand_aliasing={{}: (5, {})} | custom-call | tf_op jit(solution)/shard_map/far/pallas_call | solution.py:286
  54.2 2.3 %all-to-all-done = bf16[128,4,128]{2,1,0:T(4,128)(2,1)S(1)} async-done(((bf16[128,4,128]{2,1,0:T(4,128)(2,1)}), bf16[128,4,128]{2,1,0:T(4,128)(2,1)S(1)}, u32[]{:S(2)}, u32[]{:S(2)}) %all-to-all-start) | async-done | bytes 131104 | tf_op jit(solution)/shard_map/all_to_all | solution.py:352
  56.4 0.7 %convert_reduce_fusion = f32[4,4,128]{2,1,0:T(4,128)} fusion(bf16[128,4,128]{2,1,0:T(4,128)(2,1)S(1)} %all-to-all-done), kind=kLoop, calls=%fused_computation | loop fusion | flops 129024 | bytes 139264 | tf_op jit(solution)/shard_map/reduce_sum | solution.py:354
  (10 shorter events, 0.1 us)
Async XLA Ops:
  1.8 13.4 %collective-permute-start.2 = (s16[640,128]{1,0:T(8,128)(2,1)S(1)}, s16[640,128]{1,0:T(8,128)(2,1)S(1)}, u32[]{:S(2)}, u32[]{:S(2)}) collective-permute-start(s16[640,128]{1,0:T(8,128)(2,1)S(1)} %get-tuple-element.14.refs_0_), channel_id=1, source_target_pairs={{24,0},{0,8},{8,16},{16,24},{25,1},{1,9},{9,17},{17,25},{26,2},{2,... | collective-permute-start | bytes 491528 | tf_op jit(solution)/shard_map/ppermute | solution.py:300
  3.5 13.9 %collective-permute-start.1 = (s16[640,128]{1,0:T(8,128)(2,1)S(1)}, s16[640,128]{1,0:T(8,128)(2,1)S(1)}, u32[]{:S(2)}, u32[]{:S(2)}) collective-permute-start(s16[640,128]{1,0:T(8,128)(2,1)S(1)} %get-tuple-element.14.refs_0_), channel_id=1, source_target_pairs={{16,0},{24,8},{0,16},{8,24},{17,1},{25,9},{1,17},{9,25},{18,2},{26... | collective-permute-start | bytes 491528 | tf_op jit(solution)/shard_map/ppermute | solution.py:300
  6.2 17.9 %collective-permute-start.6 = (s16[640,128]{1,0:T(8,128)(2,1)S(1)}, s16[640,128]{1,0:T(8,128)(2,1)S(1)}, u32[]{:S(2)}, u32[]{:S(2)}) collective-permute-start(s16[640,128]{1,0:T(8,128)(2,1)S(1)} %get-tuple-element.14.refs_0_), channel_id=1, source_target_pairs={{4,0},{5,1},{6,2},{7,3},{0,4},{1,5},{2,6},{3,7},{12,8},{13,9},{14,... | collective-permute-start | bytes 491528 | tf_op jit(solution)/shard_map/ppermute | solution.py:300
  10.1 11.2 %collective-permute-start = (s16[640,128]{1,0:T(8,128)(2,1)S(1)}, s16[640,128]{1,0:T(8,128)(2,1)S(1)}, u32[]{:S(2)}, u32[]{:S(2)}) collective-permute-start(s16[640,128]{1,0:T(8,128)(2,1)S(1)} %get-tuple-element.14.refs_0_), channel_id=1, source_target_pairs={{8,0},{16,8},{24,16},{0,24},{9,1},{17,9},{25,17},{1,25},{10,2},{18... | collective-permute-start | bytes 491528 | tf_op jit(solution)/shard_map/ppermute | solution.py:300
  11.5 12.6 %collective-permute-start.5 = (s16[640,128]{1,0:T(8,128)(2,1)S(1)}, s16[640,128]{1,0:T(8,128)(2,1)S(1)}, u32[]{:S(2)}, u32[]{:S(2)}) collective-permute-start(s16[640,128]{1,0:T(8,128)(2,1)S(1)} %get-tuple-element.14.refs_0_), channel_id=1, source_target_pairs={{5,0},{6,1},{7,2},{0,3},{1,4},{2,5},{3,6},{4,7},{13,8},{14,9},{15,... | collective-permute-start | bytes 491528 | tf_op jit(solution)/shard_map/ppermute | solution.py:300
  15.2 9.0 %collective-permute-start.4 = (s16[640,128]{1,0:T(8,128)(2,1)S(1)}, s16[640,128]{1,0:T(8,128)(2,1)S(1)}, u32[]{:S(2)}, u32[]{:S(2)}) collective-permute-start(s16[640,128]{1,0:T(8,128)(2,1)S(1)} %get-tuple-element.14.refs_0_), channel_id=1, source_target_pairs={{2,0},{3,1},{4,2},{5,3},{6,4},{7,5},{0,6},{1,7},{10,8},{11,9},{12,... | collective-permute-start | bytes 491528 | tf_op jit(solution)/shard_map/ppermute | solution.py:300
  17.4 6.8 %collective-permute-start.3 = (s16[640,128]{1,0:T(8,128)(2,1)S(1)}, s16[640,128]{1,0:T(8,128)(2,1)S(1)}, u32[]{:S(2)}, u32[]{:S(2)}) collective-permute-start(s16[640,128]{1,0:T(8,128)(2,1)S(1)} %get-tuple-element.14.refs_0_), channel_id=1, source_target_pairs={{1,0},{2,1},{3,2},{4,3},{5,4},{6,5},{7,6},{0,7},{9,8},{10,9},{11,1... | collective-permute-start | bytes 491528 | tf_op jit(solution)/shard_map/ppermute | solution.py:300
  24.2 6.9 %collective-permute-start.7 = (s16[8,128,128]{2,1,0:T(8,128)(2,1)S(1)}, s16[8,128,128]{2,1,0:T(8,128)(2,1)S(1)}, u32[]{:S(2)}, u32[]{:S(2)}) collective-permute-start(s16[8,128,128]{2,1,0:T(8,128)(2,1)S(1)} %stack.1.a0), channel_id=1, source_target_pairs={{64,0},{96,32},{0,64},{32,96},{65,1},{97,33},{1,65},{33,97},{66,2}... | collective-permute-start | bytes 786440 | tf_op jit(solution)/shard_map/ppermute | solution.py:304
  28.8 2.4 %collective-permute-start.8 = (s16[8,128,128]{2,1,0:T(8,128)(2,1)S(1)}, s16[8,128,128]{2,1,0:T(8,128)(2,1)S(1)}, u32[]{:S(2)}, u32[]{:S(2)}) collective-permute-start(s16[8,128,128]{2,1,0:T(8,128)(2,1)S(1)} %stack.1.a0), channel_id=1, source_target_pairs={{32,0},{0,32},{96,64},{64,96},{33,1},{1,33},{97,65},{65,97},{34,2}... | collective-permute-start | bytes 786440 | tf_op jit(solution)/shard_map/ppermute | solution.py:304
  31.2 1.5 %collective-permute-start.9 = (s16[8,128,128]{2,1,0:T(8,128)(2,1)S(1)}, s16[8,128,128]{2,1,0:T(8,128)(2,1)S(1)}, u32[]{:S(2)}, u32[]{:S(2)}) collective-permute-start(s16[8,128,128]{2,1,0:T(8,128)(2,1)S(1)} %collective-permute-done.7.a1), channel_id=1, source_target_pairs={{32,0},{0,32},{96,64},{64,96},{33,1},{1,33},{97,65},{65,97},{34,2}... | collective-permute-start | bytes 786440 | tf_op jit(solution)/shard_map/ppermute | solution.py:304
  40.1 16.3 %all-to-all-start = ((bf16[128,4,128]{2,1,0:T(4,128)(2,1)}), bf16[128,4,128]{2,1,0:T(4,128)(2,1)S(1)}, u32[]{:S(2)}, u32[]{:S(2)}) async-start(bf16[128,4,128]{2,1,0:T(4,128)(2,1)} %bitcast.1), calls=%async_computation | async-start | bytes 262144 | tf_op jit(solution)/shard_map/all_to_all | solution.py:352
  46.9 6.0 %collective-permute-start.10 = (s16[4,3,32,128]{3,2,1,0:T(8,128)(2,1)S(1)}, s16[4,3,32,128]{3,2,1,0:T(8,128)(2,1)S(1)}, u32[]{:S(2)}, u32[]{:S(2)}) collective-permute-start(s16[4,3,32,128]{3,2,1,0:T(8,128)(2,1)S(1)} %pack.1), channel_id=1, source_target_pairs={{2,0},{3,1},{4,2},{5,3},{6,4},{7,5},{0,6},{1,7},{10,8},{11,9},{12,... | collective-permute-start | bytes 294920 | tf_op jit(solution)/shard_map/ppermute | solution.py:300
where the time goes:
time: 57.6 us; the launch traced here: 57.1 us
  starting transfers between devices  29 us (50%)
  Pallas kernels  19.1 us (33%)
  waiting for transfers between devices  7.6 us (13%)
  between operations  0.75 us (1%)
  other arithmetic  0.66 us (1%)
    ppermute x8, starting transfers between devices, from_offset(): lax.ppermute(value, axis, [((i + offset) % size, i) for i in range(size)])  21.4 us
    pallas_call x3, Pallas kernels, steer(): pl.pallas_call(steer_kernel, out_shape=pltpu.VMEM((F, 2, n, NPT, NST), jn...  7.56 us
    pallas_call x1, Pallas kernels, beams(): pl.pallas_call(beam_kernel, out_shape=pltpu.VMEM((F, 32, 4, NST), jnp.bfl...  7.38 us
    all_to_all x1, starting transfers between devices, local(): shares = lax.all_to_all(partial.reshape(128, 4, NST), ALL, 0, 0, tiled=True)  6.73 us
    ppermute x3, waiting for transfers between devices, from_partner(): return lax.ppermute(value, 'win', [(i ^ bit, i) for i in range(4)])  3.82 us
    all_to_all x1, waiting for transfers between devices, local(): shares = lax.all_to_all(partial.reshape(128, 4, NST), ALL, 0, 0, tiled=True)  2.27 us
    pallas_call x1, Pallas kernels, near_tile(): pl.pallas_call(near_kernel, in_specs=vmem(4), out_specs=ANY, scratch_shap...  1.66 us
    ppermute x8, waiting for transfers between devices, from_offset(): lax.ppermute(value, axis, [((i + offset) % size, i) for i in range(size)])  1.51 us
  transfers between devices with their start and end apart: 12, of which 5 were waited for; matrix products, arithmetic and copies ran while one was open for 0% of the time, Pallas kernels for 18%

commit v1 on v0

--- a/solution.py
+++ b/solution.py
@@ -15,7 +15,7 @@
 ROW_OFF = (0, 1, 2, -3, 4)
 WEIGHT = ((1, 2, 1), (2, 2, 2, 2), (2, 2, 2, 2), (2, 2, 2, 2), (1, 2, 1))
 RELAY = (4, 6, 7)
-SENDS = (('srow', 3), ('srow', 2), ('scol', 2), ('srow', 1), ('scol', 4), ('scol', -3), ('scol', 1))
+SENDS = (('srow', 3), ('srow', 2), ('srow', 1), ('scol', 2), ('scol', 4), ('scol', -3), ('scol', 1))
 ROUND = 12582912.0
 AHEAD = 1
 
@@ -133,9 +133,9 @@
         x = jnp.concatenate(parts, axis=0)
         z = jnp.concatenate([q for v in parts for q in (v[16:32], -v[0:16])], axis=0)
         right = jnp.concatenate([x, z], axis=1)
+        whole = jnp.dot(cols[f % 2, :len(WEIGHT[k]) * NST, :], right, preferred_element_type=jnp.float32)
         for j, weight in enumerate(WEIGHT[k]):
-            at = slice(j * NST, (j + 1) * NST)
-            cross = jnp.dot(cols[f % 2, at, :], right, preferred_element_type=jnp.float32)
+            cross = whole[j * NST:(j + 1) * NST]
             re = cross[:, :NST]
             im = cross[:, NST:]
             inverse = lax.rsqrt(re * re + im * im + 64.0)

time: 57.6 us -> 57.6 us (level)
  no operation moved by 1% of the time
where the time goes in v1:
time: 57.6 us; the launch traced here: 57.1 us
  starting transfers between devices  29 us (50%)
  Pallas kernels  19.1 us (33%)
  waiting for transfers between devices  7.6 us (13%)
  between operations  0.75 us (1%)
  other arithmetic  0.66 us (1%)
    ppermute x8, starting transfers between devices, from_offset(): lax.ppermute(value, axis, [((i + offset) % size, i) for i in range(size)])  21.4 us
    pallas_call x3, Pallas kernels, steer(): pl.pallas_call(steer_kernel, out_shape=pltpu.VMEM((F, 2, n, NPT, NST), jn...  7.56 us
    pallas_call x1, Pallas kernels, beams(): pl.pallas_call(beam_kernel, out_shape=pltpu.VMEM((F, 32, 4, NST), jnp.bfl...  7.36 us
    all_to_all x1, starting transfers between devices, local(): shares = lax.all_to_all(partial.reshape(128, 4, NST), ALL, 0, 0, tiled=True)  6.73 us
    ppermute x3, waiting for transfers between devices, from_partner(): return lax.ppermute(value, 'win', [(i ^ bit, i) for i in range(4)])  3.82 us
    all_to_all x1, waiting for transfers between devices, local(): shares = lax.all_to_all(partial.reshape(128, 4, NST), ALL, 0, 0, tiled=True)  2.26 us
    pallas_call x1, Pallas kernels, near_tile(): pl.pallas_call(near_kernel, in_specs=vmem(4), out_specs=ANY, scratch_shap...  1.66 us
    ppermute x8, waiting for transfers between devices, from_offset(): lax.ppermute(value, axis, [((i + offset) % size, i) for i in range(size)])  1.51 us
  transfers between devices with their start and end apart: 12, of which 5 were waited for; matrix products, arithmetic and copies ran while one was open for 0% of the time, Pallas kernels for 18%

profile of v1, /device:TPU:0, one launch (start us, length us, event | category | flops | bytes accessed | tf_op | source)
XLA Modules:
  0.0 57.1 jit_solution(2975974345980748340)
XLA Ops:
  0.6 1.2 %prep.1 = (s16[640,128]{1,0:T(8,128)(2,1)S(1)}, f32[4,8,128]{2,1,0:T(8,128)S(1)}) custom-call(f32[4,2,16,128]{3,2,1,0:T(8,128)} %spectra_hbm.1, s32[128,512]{1,0:T(8,128)} %travel_hbm.1, s32[4]{0:T(128)} %bins_hbm.1), custom_call_target="tpu_custom_call" | custom-call | tf_op jit(solution)/shard_map/prep/pallas_call | solution.py:316
  1.8 1.7 %collective-permute-start.2 = (s16[640,128]{1,0:T(8,128)(2,1)S(1)}, s16[640,128]{1,0:T(8,128)(2,1)S(1)}, u32[]{:S(2)}, u32[]{:S(2)}) collective-permute-start(s16[640,128]{1,0:T(8,128)(2,1)S(1)} %get-tuple-element.14.refs_0_), channel_id=1, source_target_pairs={{24,0},{0,8},{8,16},{16,24},{25,1},{1,9},{9,17},{17,25},{26,2},{2,... | collective-permute-start | bytes 491528 | tf_op jit(solution)/shard_map/ppermute | solution.py:300
  3.5 2.7 %collective-permute-start.1 = (s16[640,128]{1,0:T(8,128)(2,1)S(1)}, s16[640,128]{1,0:T(8,128)(2,1)S(1)}, u32[]{:S(2)}, u32[]{:S(2)}) collective-permute-start(s16[640,128]{1,0:T(8,128)(2,1)S(1)} %get-tuple-element.14.refs_0_), channel_id=1, source_target_pairs={{16,0},{24,8},{0,16},{8,24},{17,1},{25,9},{1,17},{9,25},{18,2},{26... | collective-permute-start | bytes 491528 | tf_op jit(solution)/shard_map/ppermute | solution.py:300
  6.2 3.9 %collective-permute-start.6 = (s16[640,128]{1,0:T(8,128)(2,1)S(1)}, s16[640,128]{1,0:T(8,128)(2,1)S(1)}, u32[]{:S(2)}, u32[]{:S(2)}) collective-permute-start(s16[640,128]{1,0:T(8,128)(2,1)S(1)} %get-tuple-element.14.refs_0_), channel_id=1, source_target_pairs={{4,0},{5,1},{6,2},{7,3},{0,4},{1,5},{2,6},{3,7},{12,8},{13,9},{14,... | collective-permute-start | bytes 491528 | tf_op jit(solution)/shard_map/ppermute | solution.py:300
  10.1 1.4 %collective-permute-start = (s16[640,128]{1,0:T(8,128)(2,1)S(1)}, s16[640,128]{1,0:T(8,128)(2,1)S(1)}, u32[]{:S(2)}, u32[]{:S(2)}) collective-permute-start(s16[640,128]{1,0:T(8,128)(2,1)S(1)} %get-tuple-element.14.refs_0_), channel_id=1, source_target_pairs={{8,0},{16,8},{24,16},{0,24},{9,1},{17,9},{25,17},{1,25},{10,2},{18... | collective-permute-start | bytes 491528 | tf_op jit(solution)/shard_map/ppermute | solution.py:300
  11.5 3.6 %collective-permute-start.5 = (s16[640,128]{1,0:T(8,128)(2,1)S(1)}, s16[640,128]{1,0:T(8,128)(2,1)S(1)}, u32[]{:S(2)}, u32[]{:S(2)}) collective-permute-start(s16[640,128]{1,0:T(8,128)(2,1)S(1)} %get-tuple-element.14.refs_0_), channel_id=1, source_target_pairs={{5,0},{6,1},{7,2},{0,3},{1,4},{2,5},{3,6},{4,7},{13,8},{14,9},{15,... | collective-permute-start | bytes 491528 | tf_op jit(solution)/shard_map/ppermute | solution.py:300
  15.2 2.2 %collective-permute-start.4 = (s16[640,128]{1,0:T(8,128)(2,1)S(1)}, s16[640,128]{1,0:T(8,128)(2,1)S(1)}, u32[]{:S(2)}, u32[]{:S(2)}) collective-permute-start(s16[640,128]{1,0:T(8,128)(2,1)S(1)} %get-tuple-element.14.refs_0_), channel_id=1, source_target_pairs={{2,0},{3,1},{4,2},{5,3},{6,4},{7,5},{0,6},{1,7},{10,8},{11,9},{12,... | collective-permute-start | bytes 491528 | tf_op jit(solution)/shard_map/ppermute | solution.py:300
  17.4 2.9 %collective-permute-start.3 = (s16[640,128]{1,0:T(8,128)(2,1)S(1)}, s16[640,128]{1,0:T(8,128)(2,1)S(1)}, u32[]{:S(2)}, u32[]{:S(2)}) collective-permute-start(s16[640,128]{1,0:T(8,128)(2,1)S(1)} %get-tuple-element.14.refs_0_), channel_id=1, source_target_pairs={{1,0},{2,1},{3,2},{4,3},{5,4},{6,5},{7,6},{0,7},{9,8},{10,9},{11,1... | collective-permute-start | bytes 491528 | tf_op jit(solution)/shard_map/ppermute | solution.py:300
  20.3 0.9 %shard_map.50.own_steer = bf16[4,2,1,512,128]{4,3,2,1,0:T(8,128)(2,1)S(1)} custom-call(f32[4,8,128]{2,1,0:T(8,128)S(1)} %get-tuple-element.15.scales, s16[640,128]{1,0:T(8,128)(2,1)S(1)} %get-tuple-element.14.refs_0_), custom_call_target="tpu_custom_call" | custom-call | tf_op jit(solution)/shard_map/pallas_call | solution.py:92
  21.3 2.8 %shard_map.51.row_steer = bf16[4,2,3,512,128]{4,3,2,1,0:T(8,128)(2,1)S(1)} custom-call(f32[4,8,128]{2,1,0:T(8,128)S(1)} %get-tuple-element.15.scales, s16[640,128]{1,0:T(8,128)(2,1)S(1)} %collective-permute-done.refs_0_.refs_1_, s16[640,128]{1,0:T(8,128)(2,1)S(1)} %collective-permute-done.1.refs_1_.refs_2_, ...), custom_call_target="tpu_custom_call" | custom-call | tf_op jit(solution)/shard_map/pallas_call | solution.py:92
  24.1 0.1 collective-permute-done.3.refs_4_.refs_0_
  24.2 0.8 %collective-permute-start.7 = (s16[8,128,128]{2,1,0:T(8,128)(2,1)S(1)}, s16[8,128,128]{2,1,0:T(8,128)(2,1)S(1)}, u32[]{:S(2)}, u32[]{:S(2)}) collective-permute-start(s16[8,128,128]{2,1,0:T(8,128)(2,1)S(1)} %stack.1.a0), channel_id=1, source_target_pairs={{64,0},{96,32},{0,64},{32,96},{65,1},{97,33},{1,65},{33,97},{66,2}... | collective-permute-start | bytes 786440 | tf_op jit(solution)/shard_map/ppermute | solution.py:304
  25.0 3.8 %shard_map.52.col_steer = bf16[4,2,4,512,128]{4,3,2,1,0:T(8,128)(2,1)S(1)} custom-call(f32[4,8,128]{2,1,0:T(8,128)S(1)} %get-tuple-element.15.scales, s16[640,128]{1,0:T(8,128)(2,1)S(1)} %collective-permute-done.3.refs_4_.refs_0_, s16[640,128]{1,0:T(8,128)(2,1)S(1)} %collective-permute-done.4.refs_5_.refs_1_, ...), custom_call_target="tpu_custom_call" | custom-call | tf_op jit(solution)/shard_map/pallas_call | solution.py:92
  28.8 0.1 collective-permute-start.8
  28.9 2.3 %collective-permute-done.7.a1 = s16[8,128,128]{2,1,0:T(8,128)(2,1)S(1)} collective-permute-done((s16[8,128,128]{2,1,0:T(8,128)(2,1)S(1)}, s16[8,128,128]{2,1,0:T(8,128)(2,1)S(1)}, u32[]{:S(2)}, u32[]{:S(2)}) %collective-permute-start.7) | collective-permute-done | bytes 262176 | tf_op jit(solution)/shard_map/ppermute | solution.py:304
  31.2 1.5 %collective-permute-done.9.a3 = s16[8,128,128]{2,1,0:T(8,128)(2,1)S(1)} collective-permute-done((s16[8,128,128]{2,1,0:T(8,128)(2,1)S(1)}, s16[8,128,128]{2,1,0:T(8,128)(2,1)S(1)}, u32[]{:S(2)}, u32[]{:S(2)}) %collective-permute-start.9) | collective-permute-done | bytes 262176 | tf_op jit(solution)/shard_map/ppermute | solution.py:304
  32.7 7.4 %beams.1 = bf16[4,32,4,128]{3,2,1,0:T(4,128)(2,1)} custom-call(bf16[4,2,1,512,128]{4,3,2,1,0:T(8,128)(2,1)S(1)} %shard_map.50.own_steer, bf16[4,2,4,512,128]{4,3,2,1,0:T(8,128)(2,1)S(1)} %shard_map.52.col_steer, bf16[4,2,3,512,128]{4,3,2,1,0:T(8,128)(2,1)S(1)} %shard_map.51.row_steer, s16[8,128,128]{2,1,0:T(8,128)(2,1)S(1)} %stack.1.a0, ...), custom_call_target="tpu_custom_call" | custom-call | tf_op jit(solution)/shard_map/beams/pallas_call | solution.py:179
  40.1 6.7 %all-to-all-start = ((bf16[128,4,128]{2,1,0:T(4,128)(2,1)}), bf16[128,4,128]{2,1,0:T(4,128)(2,1)S(1)}, u32[]{:S(2)}, u32[]{:S(2)}) async-start(bf16[128,4,128]{2,1,0:T(4,128)(2,1)} %bitcast.1), calls=%async_computation | async-start | bytes 262144 | tf_op jit(solution)/shard_map/all_to_all | solution.py:352
  46.8 2.9 %collective-permute-start.10 = (s16[4,3,32,128]{3,2,1,0:T(8,128)(2,1)S(1)}, s16[4,3,32,128]{3,2,1,0:T(8,128)(2,1)S(1)}, u32[]{:S(2)}, u32[]{:S(2)}) collective-permute-start(s16[4,3,32,128]{3,2,1,0:T(8,128)(2,1)S(1)} %pack.1), channel_id=1, source_target_pairs={{2,0},{3,1},{4,2},{5,3},{6,4},{7,5},{0,6},{1,7},{10,8},{11,9},{12,... | collective-permute-start | bytes 294920 | tf_op jit(solution)/shard_map/ppermute | solution.py:300
  49.7 1.7 %near.1.old = bf16[2,4096,128]{2,1,0:T(8,128)(2,1)} custom-call(s16[8,128,128]{2,1,0:T(8,128)(2,1)S(1)} %stack.1.a0, s16[8,128,128]{2,1,0:T(8,128)(2,1)S(1)} %collective-permute-done.7.a1, s16[8,128,128]{2,1,0:T(8,128)(2,1)S(1)} %collective-permute-done.8.a2, s16[8,128,128]{2,1,0:T(8,128)(2,1)S(1)} %collective-permute-done.9.a3), custom_call_target="tpu_custom_call" | custom-call | tf_op jit(solution)/shard_map/near/pallas_call | solution.py:274
  51.4 1.4 %collective-permute-done.10.rows = s16[4,3,32,128]{3,2,1,0:T(8,128)(2,1)S(1)} collective-permute-done((s16[4,3,32,128]{3,2,1,0:T(8,128)(2,1)S(1)}, s16[4,3,32,128]{3,2,1,0:T(8,128)(2,1)S(1)}, u32[]{:S(2)}, u32[]{:S(2)}) %collective-permute-start.10) | collective-permute-done | bytes 98336 | tf_op jit(solution)/shard_map/ppermute | solution.py:300
  52.8 1.3 %far.1 = bf16[2,4096,128]{2,1,0:T(8,128)(2,1)} custom-call(s16[4,3,32,128]{3,2,1,0:T(8,128)(2,1)S(1)} %collective-permute-done.10.rows, s16[8,128,128]{2,1,0:T(8,128)(2,1)S(1)} %stack.1.a0, s16[8,128,128]{2,1,0:T(8,128)(2,1)S(1)} %collective-permute-done.7.a1, s16[8,128,128]{2,1,0:T(8,128)(2,1)S(1)} %collective-permute-done.8.a2, ...), custom_call_target="tpu_custom_call", output_to_operand_aliasing={{}: (5, {})} | custom-call | tf_op jit(solution)/shard_map/far/pallas_call | solution.py:286
  54.1 2.3 %all-to-all-done = bf16[128,4,128]{2,1,0:T(4,128)(2,1)S(1)} async-done(((bf16[128,4,128]{2,1,0:T(4,128)(2,1)}), bf16[128,4,128]{2,1,0:T(4,128)(2,1)S(1)}, u32[]{:S(2)}, u32[]{:S(2)}) %all-to-all-start) | async-done | bytes 131104 | tf_op jit(solution)/shard_map/all_to_all | solution.py:352
  56.4 0.7 %convert_reduce_fusion = f32[4,4,128]{2,1,0:T(4,128)} fusion(bf16[128,4,128]{2,1,0:T(4,128)(2,1)S(1)} %all-to-all-done), kind=kLoop, calls=%fused_computation | loop fusion | flops 129024 | bytes 139264 | tf_op jit(solution)/shard_map/reduce_sum | solution.py:354
  (10 shorter events, 0.1 us)
Async XLA Ops:
  1.8 13.4 %collective-permute-start.2 = (s16[640,128]{1,0:T(8,128)(2,1)S(1)}, s16[640,128]{1,0:T(8,128)(2,1)S(1)}, u32[]{:S(2)}, u32[]{:S(2)}) collective-permute-start(s16[640,128]{1,0:T(8,128)(2,1)S(1)} %get-tuple-element.14.refs_0_), channel_id=1, source_target_pairs={{24,0},{0,8},{8,16},{16,24},{25,1},{1,9},{9,17},{17,25},{26,2},{2,... | collective-permute-start | bytes 491528 | tf_op jit(solution)/shard_map/ppermute | solution.py:300
  3.5 13.9 %collective-permute-start.1 = (s16[640,128]{1,0:T(8,128)(2,1)S(1)}, s16[640,128]{1,0:T(8,128)(2,1)S(1)}, u32[]{:S(2)}, u32[]{:S(2)}) collective-permute-start(s16[640,128]{1,0:T(8,128)(2,1)S(1)} %get-tuple-element.14.refs_0_), channel_id=1, source_target_pairs={{16,0},{24,8},{0,16},{8,24},{17,1},{25,9},{1,17},{9,25},{18,2},{26... | collective-permute-start | bytes 491528 | tf_op jit(solution)/shard_map/ppermute | solution.py:300
  6.2 17.9 %collective-permute-start.6 = (s16[640,128]{1,0:T(8,128)(2,1)S(1)}, s16[640,128]{1,0:T(8,128)(2,1)S(1)}, u32[]{:S(2)}, u32[]{:S(2)}) collective-permute-start(s16[640,128]{1,0:T(8,128)(2,1)S(1)} %get-tuple-element.14.refs_0_), channel_id=1, source_target_pairs={{4,0},{5,1},{6,2},{7,3},{0,4},{1,5},{2,6},{3,7},{12,8},{13,9},{14,... | collective-permute-start | bytes 491528 | tf_op jit(solution)/shard_map/ppermute | solution.py:300
  10.1 11.2 %collective-permute-start = (s16[640,128]{1,0:T(8,128)(2,1)S(1)}, s16[640,128]{1,0:T(8,128)(2,1)S(1)}, u32[]{:S(2)}, u32[]{:S(2)}) collective-permute-start(s16[640,128]{1,0:T(8,128)(2,1)S(1)} %get-tuple-element.14.refs_0_), channel_id=1, source_target_pairs={{8,0},{16,8},{24,16},{0,24},{9,1},{17,9},{25,17},{1,25},{10,2},{18... | collective-permute-start | bytes 491528 | tf_op jit(solution)/shard_map/ppermute | solution.py:300
  11.5 12.6 %collective-permute-start.5 = (s16[640,128]{1,0:T(8,128)(2,1)S(1)}, s16[640,128]{1,0:T(8,128)(2,1)S(1)}, u32[]{:S(2)}, u32[]{:S(2)}) collective-permute-start(s16[640,128]{1,0:T(8,128)(2,1)S(1)} %get-tuple-element.14.refs_0_), channel_id=1, source_target_pairs={{5,0},{6,1},{7,2},{0,3},{1,4},{2,5},{3,6},{4,7},{13,8},{14,9},{15,... | collective-permute-start | bytes 491528 | tf_op jit(solution)/shard_map/ppermute | solution.py:300
  15.2 9.0 %collective-permute-start.4 = (s16[640,128]{1,0:T(8,128)(2,1)S(1)}, s16[640,128]{1,0:T(8,128)(2,1)S(1)}, u32[]{:S(2)}, u32[]{:S(2)}) collective-permute-start(s16[640,128]{1,0:T(8,128)(2,1)S(1)} %get-tuple-element.14.refs_0_), channel_id=1, source_target_pairs={{2,0},{3,1},{4,2},{5,3},{6,4},{7,5},{0,6},{1,7},{10,8},{11,9},{12,... | collective-permute-start | bytes 491528 | tf_op jit(solution)/shard_map/ppermute | solution.py:300
  17.4 6.8 %collective-permute-start.3 = (s16[640,128]{1,0:T(8,128)(2,1)S(1)}, s16[640,128]{1,0:T(8,128)(2,1)S(1)}, u32[]{:S(2)}, u32[]{:S(2)}) collective-permute-start(s16[640,128]{1,0:T(8,128)(2,1)S(1)} %get-tuple-element.14.refs_0_), channel_id=1, source_target_pairs={{1,0},{2,1},{3,2},{4,3},{5,4},{6,5},{7,6},{0,7},{9,8},{10,9},{11,1... | collective-permute-start | bytes 491528 | tf_op jit(solution)/shard_map/ppermute | solution.py:300
  24.2 6.9 %collective-permute-start.7 = (s16[8,128,128]{2,1,0:T(8,128)(2,1)S(1)}, s16[8,128,128]{2,1,0:T(8,128)(2,1)S(1)}, u32[]{:S(2)}, u32[]{:S(2)}) collective-permute-start(s16[8,128,128]{2,1,0:T(8,128)(2,1)S(1)} %stack.1.a0), channel_id=1, source_target_pairs={{64,0},{96,32},{0,64},{32,96},{65,1},{97,33},{1,65},{33,97},{66,2}... | collective-permute-start | bytes 786440 | tf_op jit(solution)/shard_map/ppermute | solution.py:304
  28.8 2.4 %collective-permute-start.8 = (s16[8,128,128]{2,1,0:T(8,128)(2,1)S(1)}, s16[8,128,128]{2,1,0:T(8,128)(2,1)S(1)}, u32[]{:S(2)}, u32[]{:S(2)}) collective-permute-start(s16[8,128,128]{2,1,0:T(8,128)(2,1)S(1)} %stack.1.a0), channel_id=1, source_target_pairs={{32,0},{0,32},{96,64},{64,96},{33,1},{1,33},{97,65},{65,97},{34,2}... | collective-permute-start | bytes 786440 | tf_op jit(solution)/shard_map/ppermute | solution.py:304
  31.2 1.5 %collective-permute-start.9 = (s16[8,128,128]{2,1,0:T(8,128)(2,1)S(1)}, s16[8,128,128]{2,1,0:T(8,128)(2,1)S(1)}, u32[]{:S(2)}, u32[]{:S(2)}) collective-permute-start(s16[8,128,128]{2,1,0:T(8,128)(2,1)S(1)} %collective-permute-done.7.a1), channel_id=1, source_target_pairs={{32,0},{0,32},{96,64},{64,96},{33,1},{1,33},{97,65},{65,97},{34,2}... | collective-permute-start | bytes 786440 | tf_op jit(solution)/shard_map/ppermute | solution.py:304
  40.1 16.3 %all-to-all-start = ((bf16[128,4,128]{2,1,0:T(4,128)(2,1)}), bf16[128,4,128]{2,1,0:T(4,128)(2,1)S(1)}, u32[]{:S(2)}, u32[]{:S(2)}) async-start(bf16[128,4,128]{2,1,0:T(4,128)(2,1)} %bitcast.1), calls=%async_computation | async-start | bytes 262144 | tf_op jit(solution)/shard_map/all_to_all | solution.py:352
  46.8 6.0 %collective-permute-start.10 = (s16[4,3,32,128]{3,2,1,0:T(8,128)(2,1)S(1)}, s16[4,3,32,128]{3,2,1,0:T(8,128)(2,1)S(1)}, u32[]{:S(2)}, u32[]{:S(2)}) collective-permute-start(s16[4,3,32,128]{3,2,1,0:T(8,128)(2,1)S(1)} %pack.1), channel_id=1, source_target_pairs={{2,0},{3,1},{4,2},{5,3},{6,4},{7,5},{0,6},{1,7},{10,8},{11,9},{12,... | collective-permute-start | bytes 294920 | tf_op jit(solution)/shard_map/ppermute | solution.py:300
